TPU v7x, 32 devices: a whole 2x2x4 slice. The times are simulated.
32 devices in a mesh: gx: 2 (over x), yz: 16 (over z, y, core).
Axes of the slice: x: 2, y: 2, z: 4, core: 2. Of those that a mesh axis runs over, the one named last changes fastest.
Arguments:
- system_source_term: float32 [320, 4096], P(None, ('gx', 'yz')), may hold values from -200 to 200
- mass_plus_source: float32 [320, 4096], P(None, ('gx', 'yz')), may hold values from 1 to 4
- lifted_upwind_coupling: float32 [480, 4096], P(None, ('gx', 'yz')), may hold values from 0.5 to 2
- frozen_direction_derivative: float32 [75, 4096], P(None, ('gx', 'yz')), may hold values from -3 to 3
- first_solve_matrix: float32 [320, 320], replicated, may hold values from -0.3125 to 0.3125
- final_solve_matrix: float32 [320, 320], replicated, may hold values from -0.3125 to 0.3125
- middle_cell_matrices: float32 [320, 4096], P(None, ('gx', 'yz')), may hold values from 0.3 to 3
- adjacent_table_slots: int32 [6, 4096], P(None, ('gx', 'yz')), may hold values from 0 to 1264, as said below
- plane_outgoing_cells: int32 [32, 2, 16], P(('gx', 'yz')), may hold values from 0 to 127
- band_outgoing_cells: int32 [32, 2, 16], P(('gx', 'yz')), may hold values from 0 to 127
- small_side_table_slot: int32 [32, 352], P(('gx', 'yz')), may hold values from 0 to 768, as said below
- proprietor_mortar_index: int32 [32, 352], P(('gx', 'yz')), may hold values from 0 to 80, as said below
- outgoing_quadrant_index: int32 [32, 352], P(('gx', 'yz')), may hold values from 0 to 3, as said below
- incoming_mortar_index: int32 [32, 352], P(('gx', 'yz')), may hold values from 0 to 80
- incoming_quadrant_index: int32 [32, 352], P(('gx', 'yz')), may hold values from 0 to 3, as said below
- coarse_mortar_table_slot: int32 [32, 80], P(('gx', 'yz')), may hold values from 0 to 767
Outputs:
- newton_update: float32 [320, 4096], P(None, ('gx', 'yz'))
Inputs may be any that keep to these rules, and one draw needn't show every extreme that they name: `adjacent_table_slots`: column of the neighbour trace in the device's table; 1264 marks a boundary face. `small_side_table_slot`: 768 marks an empty slot, exactly where proprietor_mortar_index is 80. Send slot (m, c) of device (g, k) and receive slot (k, c) of device (g, m) hold the same tile: there proprietor_mortar_index, outgoing_quadrant_index equal incoming_mortar_index, incoming_quadrant_index here; 80 marks an empty slot; no position of an owner's hanging face is sent twice; the live hanging faces of an owner are its first ones; from one device to one owner go at most 22 tiles, a bound reached in every draw; in each gx plane one owner receives 4 * 80 tiles. `outgoing_quadrant_index`: 0 in empty slots. `incoming_quadrant_index`: 0 in empty slots.
All inputs are finite; a program needn't handle non-finite values.
Results may differ from a plain program's by a relative error of at most 0.0003.
Values sent between devices are 32-bit elements; how exact they have to be, the bound alone decides.
No kernel may reach another device: no remote copies, remote signals or barrier semaphores. Data moves between devices by JAX's collectives and lax.ppermute only.
A program may use at most 64 MiB of HBM per device.

v0:
```python
import jax
import jax.numpy as jnp
import numpy as np
from jax import lax
from jax.sharding import PartitionSpec as P

ITERS = 2
maximum_depth = lax.Precision.HIGHEST
epsilon = 1e-06


def with_halo(shard, sides, width, wrap):
    for axis, dim in sides:
        size, length = (lax.axis_size(axis), shard.shape[dim])
        up = [(i, (i + 1) % size) for i in range(size if wrap else size - 1)]
        down = [(j, i) for i, j in up]
        last = lax.slice_in_dim(shard, length - width, length, axis=dim)
        leading = lax.slice_in_dim(shard, 0, width, axis=dim)
        before = lax.ppermute(last, axis, up)
        after = lax.ppermute(leading, axis, down)
        shard = jnp.concatenate([before, shard, after], axis=dim)
    return shard


def gll_tables():
    inv_root = 1.0 / np.sqrt(5.0)
    gll_points = np.array([-1.0, -inv_root, inv_root, 1.0])
    weights = np.array([1.0, 5.0, 5.0, 1.0]) / 6.0

    def lagrange(points):
        values_at = np.ones((len(points), 4))
        for table_slot_index in range(4):
            for m in range(4):
                if m != table_slot_index:
                    values_at[:, table_slot_index] = (
                        values_at[:, table_slot_index]
                        * (points - gll_points[m])
                        / (gll_points[table_slot_index] - gll_points[m])
                    )
        return values_at

    derivative = np.zeros((4, 4))
    for i in range(4):
        for table_slot_index in range(4):
            summed = 0.0
            for m in range(4):
                if m != table_slot_index:
                    product_term = 1.0 / (gll_points[table_slot_index] - gll_points[m])
                    for n in range(4):
                        if n != table_slot_index and n != m:
                            product_term = (
                                product_term
                                * (gll_points[i] - gll_points[n])
                                / (gll_points[table_slot_index] - gll_points[n])
                            )
                    summed = summed + product_term
            derivative[i, table_slot_index] = summed
    halves = [lagrange((gll_points - 1.0) / 2.0), lagrange((gll_points + 1.0) / 2.0)]
    half_projections = [
        0.5 * (1.0 / weights)[:, None] * halve.T * weights[None, :] for halve in halves
    ]
    interpolate = np.stack([np.kron(halves[q // 2], halves[q % 2]) for q in range(4)])
    projection = np.stack(
        [np.kron(half_projections[q // 2], half_projections[q % 2]) for q in range(4)]
    )
    identity_four = np.eye(4)
    node_derivative = np.stack(
        [
            np.kron(derivative, np.kron(identity_four, identity_four)),
            np.kron(identity_four, np.kron(derivative, identity_four)),
            np.kron(identity_four, np.kron(identity_four, derivative)),
        ]
    )
    selection = np.zeros((6, 16, 64))
    for face_id in range(6):
        direction = face_id // 2
        fixed_node = 0 if face_id % 2 == 0 else 3
        for first in range(4):
            for second in range(4):
                if direction == 0:
                    node = fixed_node * 16 + first * 4 + second
                elif direction == 1:
                    node = first * 16 + fixed_node * 4 + second
                else:
                    node = first * 16 + second * 4 + fixed_node
                selection[face_id, first * 4 + second, node] = 1.0
    lifting = selection.transpose(2, 0, 1)
    return (
        jnp.asarray(node_derivative, jnp.float32),
        jnp.asarray(interpolate, jnp.float32),
        jnp.asarray(projection, jnp.float32),
        jnp.asarray(selection, jnp.float32),
        jnp.asarray(lifting, jnp.float32),
    )


def own_traces(argument_array, selection):
    local_count = argument_array.shape[1]
    nodal_view = argument_array.reshape(5, 64, local_count)
    faces = jnp.einsum("fsn,ane->asfe", selection, nodal_view, precision=maximum_depth)
    return faces.reshape(80, 6 * local_count)


def jacobian(
    argument_array,
    own_faces,
    near_faces,
    mass_plus_source,
    lifted_upwind_coupling,
    frozen_direction_derivative,
    node_derivative,
    lifting,
):
    local_count = argument_array.shape[1]
    nodal_view = argument_array.reshape(5, 64, local_count)
    flux_blocks = frozen_direction_derivative.reshape(3, 5, 5, local_count)
    flux_terms = jnp.einsum("dabe,bne->dane", flux_blocks, nodal_view, precision=maximum_depth)
    derived = jnp.einsum("dmn,dane->ame", node_derivative, flux_terms, precision=maximum_depth)
    difference = (own_faces - near_faces).reshape(5, 16, 6, local_count)
    coupling = lifted_upwind_coupling.reshape(6, 5, 16, local_count)
    lifted = jnp.einsum(
        "nfs,fase,asfe->ane", lifting, coupling, difference, precision=maximum_depth
    )
    return mass_plus_source * argument_array + (derived + lifted).reshape(320, local_count)


def solve_cell_system(argument_array, first_solve_matrix, final_solve_matrix, middle_cell_matrices):
    interior_share = jnp.dot(
        first_solve_matrix,
        argument_array,
        precision=maximum_depth,
        preferred_element_type=jnp.float32,
    )
    return jnp.dot(
        final_solve_matrix,
        middle_cell_matrices * interior_share,
        precision=maximum_depth,
        preferred_element_type=jnp.float32,
    )


def mortar_sums(received, incoming_mortar_index, incoming_quadrant_index, projection, hang_count):
    slot_count = received.shape[1]
    face_values = received.reshape(5, 16, slot_count)
    candidates = jnp.einsum("qmn,anc->qamc", projection, face_values, precision=maximum_depth)
    selector_q = (
        incoming_quadrant_index[None, :] == jnp.arange(4, dtype=jnp.int32)[:, None]
    ).astype(jnp.float32)
    projected = jnp.sum(candidates * selector_q[:, None, None, :], axis=0).reshape(80, slot_count)
    onehot = (
        incoming_mortar_index[:, None] == jnp.arange(hang_count, dtype=jnp.int32)[None, :]
    ).astype(jnp.float32)
    return jnp.dot(projected, onehot, precision=maximum_depth, preferred_element_type=jnp.float32)


def fine_replies(coarse_cols, outgoing_quadrant_index, interpolate):
    slot_count = coarse_cols.shape[1]
    face_values = coarse_cols.reshape(5, 16, slot_count)
    candidates = jnp.einsum("qmn,anc->qamc", interpolate, face_values, precision=maximum_depth)
    selector_q = (
        outgoing_quadrant_index[None, :] == jnp.arange(4, dtype=jnp.int32)[:, None]
    ).astype(jnp.float32)
    return jnp.sum(candidates * selector_q[:, None, None, :], axis=0).reshape(80, slot_count)


def least_squares(beta_norm, columns):
    steps_count = len(columns)
    zero_value = jnp.zeros((), jnp.float32)
    target = [beta_norm] + [zero_value] * steps_count
    rotations = []
    upper_rows = []
    for table_slot_index in range(steps_count):
        column = list(columns[table_slot_index])
        for i in range(len(rotations)):
            cos_value, sine_value = rotations[i]
            first_new = cos_value * column[i] + sine_value * column[i + 1]
            second = cos_value * column[i + 1] - sine_value * column[i]
            column[i] = first_new
            column[i + 1] = second
        radius = jnp.sqrt(
            column[table_slot_index] * column[table_slot_index]
            + column[table_slot_index + 1] * column[table_slot_index + 1]
        )
        cos_value = column[table_slot_index] / radius
        sine_value = column[table_slot_index + 1] / radius
        column[table_slot_index] = radius
        rotations.append((cos_value, sine_value))
        target[table_slot_index + 1] = -sine_value * target[table_slot_index]
        target[table_slot_index] = cos_value * target[table_slot_index]
        upper_rows.append(column[: table_slot_index + 1])
    coeffs = [zero_value] * steps_count
    for table_slot_index in reversed(range(steps_count)):
        running = target[table_slot_index]
        for k in range(table_slot_index + 1, steps_count):
            running = running - upper_rows[k][table_slot_index] * coeffs[k]
        coeffs[table_slot_index] = running / upper_rows[table_slot_index][table_slot_index]
    return coeffs


def merged_global(partial_values):
    return lax.psum(partial_values, ("gx", "yz"))


def on_device(
    system_source_term,
    mass_plus_source,
    lifted_upwind_coupling,
    frozen_direction_derivative,
    first_solve_matrix,
    final_solve_matrix,
    middle_cell_matrices,
    adjacent_table_slots,
    plane_outgoing_cells,
    band_outgoing_cells,
    small_side_table_slot,
    proprietor_mortar_index,
    outgoing_quadrant_index,
    incoming_mortar_index,
    incoming_quadrant_index,
    coarse_mortar_table_slot,
):
    node_derivative, interpolate, projection, selection, lifting = gll_tables()
    local_count = system_source_term.shape[1]
    hang_count = coarse_mortar_table_slot.shape[1]
    halo_width = plane_outgoing_cells.shape[2]
    near_index = adjacent_table_slots.reshape(-1)
    defect_array = solve_cell_system(
        system_source_term, first_solve_matrix, final_solve_matrix, middle_cell_matrices
    )
    beta_norm = jnp.sqrt(
        merged_global(jnp.stack([jnp.sum(defect_array * defect_array)]))[0] + epsilon
    )
    arnoldi_directions = [defect_array / beta_norm]
    columns = []
    for table_slot_index in range(ITERS):
        argument_array = arnoldi_directions[table_slot_index]
        own_faces = own_traces(argument_array, selection)
        slab_buffer = jnp.stack(
            [
                jnp.take(own_faces, plane_outgoing_cells[0, 0], axis=1),
                jnp.take(own_faces, local_count + plane_outgoing_cells[0, 1], axis=1),
            ]
        ).reshape(2, 80 * halo_width)
        slab_padded = with_halo(slab_buffer, (("gx", 0),), 1, False)
        side_buffer = jnp.stack(
            [
                jnp.take(own_faces, 2 * local_count + band_outgoing_cells[0, 0], axis=1),
                jnp.take(own_faces, 3 * local_count + band_outgoing_cells[0, 1], axis=1),
            ]
        ).reshape(2, 80 * halo_width)
        side_padded = with_halo(side_buffer, (("yz", 0),), 1, True)
        fine_send = jnp.take(
            own_faces, small_side_table_slot[0], axis=1, mode="fill", fill_value=0.0
        )
        coarse = jnp.take(own_faces, coarse_mortar_table_slot[0], axis=1)
        outgoing = jnp.take(coarse, incoming_mortar_index[0], axis=1, mode="fill", fill_value=0.0)
        fine_recv = lax.all_to_all(fine_send, "yz", split_axis=1, concat_axis=1, tiled=True)
        coarse_cols = lax.all_to_all(outgoing, "yz", split_axis=1, concat_axis=1, tiled=True)
        hang_sum = mortar_sums(
            fine_recv, incoming_mortar_index[0], incoming_quadrant_index[0], projection, hang_count
        )
        replies = fine_replies(coarse_cols, outgoing_quadrant_index[0], interpolate)
        trace_table = jnp.concatenate(
            [
                own_faces,
                slab_padded[0].reshape(80, halo_width),
                slab_padded[3].reshape(80, halo_width),
                side_padded[0].reshape(80, halo_width),
                side_padded[3].reshape(80, halo_width),
                hang_sum,
                replies,
            ],
            axis=1,
        )
        near_faces = jnp.take(trace_table, near_index, axis=1, mode="fill", fill_value=0.0)
        scratch_storage = solve_cell_system(
            jacobian(
                argument_array,
                own_faces,
                near_faces,
                mass_plus_source,
                lifted_upwind_coupling,
                frozen_direction_derivative,
                node_derivative,
                lifting,
            ),
            first_solve_matrix,
            final_solve_matrix,
            middle_cell_matrices,
        )
        column = []
        locals_list = [
            jnp.sum(scratch_storage * arnoldi_directions[i]) for i in range(table_slot_index + 1)
        ] + [jnp.sum(scratch_storage * scratch_storage)]
        totals = merged_global(jnp.stack(locals_list))
        squared = totals[table_slot_index + 1]
        for i in range(table_slot_index + 1):
            coefficient = totals[i]
            scratch_storage = scratch_storage - coefficient * arnoldi_directions[i]
            squared = squared - coefficient * coefficient
            column.append(coefficient)
        new_norm = jnp.sqrt(squared + epsilon)
        column.append(new_norm)
        columns.append(column)
        arnoldi_directions.append(scratch_storage / new_norm)
    coeffs = least_squares(beta_norm, columns)
    newton_update = coeffs[0] * arnoldi_directions[0]
    table_slot_index = 1
    newton_update = newton_update + coeffs[table_slot_index] * arnoldi_directions[table_slot_index]
    return newton_update


def solution(mesh):
    return jax.shard_map(
        on_device,
        mesh=mesh,
        in_specs=(
            P(None, ("gx", "yz")),
            P(None, ("gx", "yz")),
            P(None, ("gx", "yz")),
            P(None, ("gx", "yz")),
            P(),
            P(),
            P(None, ("gx", "yz")),
            P(None, ("gx", "yz")),
            P(("gx", "yz"), None, None),
            P(("gx", "yz"), None, None),
            P(("gx", "yz"), None),
            P(("gx", "yz"), None),
            P(("gx", "yz"), None),
            P(("gx", "yz"), None),
            P(("gx", "yz"), None),
            P(("gx", "yz"), None),
        ),
        out_specs=P(None, ("gx", "yz")),
        check_vma=False,
    )
```

profile of v0, /device:TPU:14, one launch (start us, length us, event | category | flops | bytes accessed | tf_op | source)
XLA Modules:
  0.0 263.6 jit_solution(4759819469362136421)
XLA Ops:
  1.0 1.5 convolution_multiply_fusion
  2.6 2.2 multiply_reduce_fusion.3
  4.8 40.6 %psum.21 = f32[1]{0:T(128)} all-reduce(f32[1]{0:T(128)} %bitcast), channel_id=1, replica_groups=mesh['gx'=2,'yz'=16] {'gx','yz'}, use_global_device_ids=true, to_apply=%region_1.0 | all-reduce | flops 1 | bytes 8 | tf_op jit(solution)/shard_map/psum | solution.py:201
  48.4 1.3 collective-permute-start
  51.1 4.5 %collective-permute-start.1 = (f32[1,1280]{1,0:T(1,128)}, f32[1,1280]{1,0:T(1,128)S(1)}, u32[]{:S(2)}, u32[]{:S(2)}) collective-permute-start(f32[1,1280]{1,0:T(1,128)} %slice.66), channel_id=1, source_target_pairs={{16,0},{17,1},{18,2},{19,3},{20,4},{21,5},{22,6},{23,7},{24,8},{25... | collective-permute-start | bytes 15368 | tf_op jit(solution)/shard_map/ppermute | solution.py:20
  58.6 1.7 collective-permute-start.3
  62.9 7.9 %all-to-all-start = ((f32[80,16,22]{0,2,1:T(8,128)}), f32[80,16,22]{0,2,1:T(8,128)}, u32[]{:S(2)}, u32[]{:S(2)}) async-start(f32[80,16,22]{0,2,1:T(8,128)} %all_to_all.24), calls=%async_computation | async-start | bytes 393216 | tf_op jit(solution)/shard_map/all_to_all | solution.py:257
  76.8 3.7 %convolution_bitcast_fusion.1 = f32[3,5,64,128]{2,1,0,3:T(8,128)S(1)} fusion(f32[5,64,128,1]{1,0,3,2:T(8,128)} %copy.180, f32[3,5,5,128]{2,1,0,3:T(8,128)S(1)} %copy.130), kind=kOutput, calls=%fused_computation.17 | convolution fusion | flops 7372800 | bytes 693760 | tf_op jit(solution)/shard_map/dabe,bne->dane/dot_general | solution.py:117
  80.5 2.0 convolution_bitcast_fusion.13
  85.8 6.1 %all-to-all-start.1 = ((f32[80,16,22]{0,2,1:T(8,128)}), f32[80,16,22]{0,2,1:T(8,128)S(1)}, u32[]{:S(2)}, u32[]{:S(2)}) async-start(f32[80,16,22]{0,2,1:T(8,128)} %all_to_all.26), calls=%async_computation.1 | async-start | bytes 393216 | tf_op jit(solution)/shard_map/all_to_all | solution.py:258
  91.9 2.1 copy.142
  94.0 1.4 reshape.366
  95.3 2.4 all-to-all-done.1
  98.9 1.4 reshape.368
  101.0 1.3 fusion.4
  103.4 2.6 gather_fusion.7
  110.1 1.3 fusion.10
  113.2 1.3 pad_maximum_fusion
  114.5 41.6 %psum.22 = f32[2]{0:T(128)S(1)} all-reduce(f32[2]{0:T(128)S(1)} %pad_maximum_fusion), channel_id=1, replica_groups=mesh['gx'=2,'yz'=16] {'gx','yz'}, use_global_device_ids=true, to_apply=%region_6.12 | all-reduce | flops 2 | bytes 16 | tf_op jit(solution)/shard_map/psum | solution.py:201
  163.5 1.6 gather_fusion.12
  167.6 3.7 %convolution_bitcast_fusion = f32[3,5,64,128]{2,1,0,3:T(8,128)S(1)} fusion(f32[5,64,128,1]{1,0,3,2:T(8,128)} %copy.187, f32[3,5,5,128]{2,1,0,3:T(8,128)S(1)} %copy.130), kind=kOutput, calls=%fused_computation.16 | convolution fusion | flops 7372800 | bytes 693760 | tf_op jit(solution)/shard_map/dabe,bne->dane/dot_general | solution.py:117
  171.3 1.3 convolution_bitcast_fusion.10
  172.9 1.3 collective-permute-start.4
  174.4 4.5 %collective-permute-start.5 = (f32[1,1280]{1,0:T(1,128)S(1)}, f32[1,1280]{1,0:T(1,128)S(1)}, u32[]{:S(2)}, u32[]{:S(2)}) collective-permute-start(f32[1,1280]{1,0:T(1,128)S(1)} %slice.74), channel_id=1, source_target_pairs={{16,0},{17,1},{18,2},{19,3},{20,4},{21,5},{22,6},{23,7},{24,8},{25... | collective-permute-start | bytes 15368 | tf_op jit(solution)/shard_map/ppermute | solution.py:20
  179.5 1.8 collective-permute-start.7
  182.1 5.9 %all-to-all-start.2 = ((f32[80,16,22]{0,2,1:T(8,128)}), f32[80,16,22]{0,2,1:T(8,128)S(1)}, u32[]{:S(2)}, u32[]{:S(2)}) async-start(f32[80,16,22]{0,2,1:T(8,128)} %all_to_all.28), calls=%async_computation.2 | async-start | bytes 393216 | tf_op jit(solution)/shard_map/all_to_all | solution.py:257
  190.7 3.1 %all-to-all-done.2 = f32[80,16,22]{0,2,1:T(8,128)S(1)} async-done(((f32[80,16,22]{0,2,1:T(8,128)}), f32[80,16,22]{0,2,1:T(8,128)S(1)}, u32[]{:S(2)}, u32[]{:S(2)}) %all-to-all-start.2) | async-done | bytes 112672 | tf_op jit(solution)/shard_map/all_to_all | solution.py:257
  193.8 6.6 %all-to-all-start.3 = ((f32[80,16,22]{0,2,1:T(8,128)}), f32[80,16,22]{0,2,1:T(8,128)S(1)}, u32[]{:S(2)}, u32[]{:S(2)}) async-start(f32[80,16,22]{0,2,1:T(8,128)} %all_to_all.30), calls=%async_computation.3 | async-start | bytes 393216 | tf_op jit(solution)/shard_map/all_to_all | solution.py:258
  201.6 4.6 %all-to-all-done.3 = f32[80,16,22]{0,2,1:T(8,128)S(1)} async-done(((f32[80,16,22]{0,2,1:T(8,128)}), f32[80,16,22]{0,2,1:T(8,128)S(1)}, u32[]{:S(2)}, u32[]{:S(2)}) %all-to-all-start.3) | async-done | bytes 112672 | tf_op jit(solution)/shard_map/all_to_all | solution.py:258
  208.1 1.6 gather_fusion.15
  212.7 2.0 pad_maximum_fusion.1
  214.6 41.7 %psum.23 = f32[3]{0:T(128)S(1)} all-reduce(f32[3]{0:T(128)S(1)} %pad_maximum_fusion.1), channel_id=1, replica_groups=mesh['gx'=2,'yz'=16] {'gx','yz'}, use_global_device_ids=true, to_apply=%region_12.18 | all-reduce | flops 3 | bytes 24 | tf_op jit(solution)/shard_map/psum | solution.py:201
  (282 shorter events, 46.5 us)
Async XLA Ops:
  0.0 46.1 %copy-start.19 = (f32[6,16,64,1]{2,1,0,3:T(8,128)S(1)}, f32[6,16,64,1]{2,1,0,3:T(8,128)}, u32[]{:S(2)}) copy-start(f32[6,16,64,1]{2,1,0,3:T(8,128)} %constant.85) | copy-start | bytes 73732
  2.6 44.9 %copy-start.58 = (s32[1,2,16]{2,1,0:T(2,128)S(1)}, s32[1,2,16]{2,1,0:T(2,128)}, u32[]{:S(2)}) copy-start(s32[1,2,16]{2,1,0:T(2,128)} %param.39) | copy-start | bytes 388
  46.1 65.9 %copy-start.3 = (f32[128,320]{0,1:T(8,128)}, f32[128,320]{0,1:T(8,128)S(1)}, u32[]{:S(2)}) copy-start(f32[128,320]{0,1:T(8,128)S(1)} %broadcast_divide_fusion) | copy-start | bytes 491524
  46.1 9.5 %copy-start.59 = (s32[1,2,16]{2,1,0:T(2,128)S(1)}, s32[1,2,16]{2,1,0:T(2,128)}, u32[]{:S(2)}) copy-start(s32[1,2,16]{2,1,0:T(2,128)} %param.40) | copy-start | bytes 388
  46.6 13.8 %copy-start.54 = (s32[1,352]{1,0:T(1,128)S(1)}, s32[1,352]{1,0:T(1,128)}, u32[]{:S(2)}) copy-start(s32[1,352]{1,0:T(1,128)} %param.41) | copy-start | bytes 4228
  48.4 36.7 %collective-permute-start = (f32[1,1280]{1,0:T(1,128)S(1)}, f32[1,1280]{1,0:T(1,128)S(1)}, u32[]{:S(2)}, u32[]{:S(2)}) collective-permute-start(f32[1,1280]{1,0:T(1,128)S(1)} %slice.64), channel_id=1, source_target_pairs={{0,16},{1,17},{2,18},{3,19},{4,20},{5,21},{6,22},{7,23},{8,24},{9,... | collective-permute-start | bytes 15368 | tf_op jit(solution)/shard_map/ppermute | solution.py:19
  51.1 34.1 %collective-permute-start.1 = (f32[1,1280]{1,0:T(1,128)}, f32[1,1280]{1,0:T(1,128)S(1)}, u32[]{:S(2)}, u32[]{:S(2)}) collective-permute-start(f32[1,1280]{1,0:T(1,128)} %slice.66), channel_id=1, source_target_pairs={{16,0},{17,1},{18,2},{19,3},{20,4},{21,5},{22,6},{23,7},{24,8},{25... | collective-permute-start | bytes 15368 | tf_op jit(solution)/shard_map/ppermute | solution.py:20
  57.2 28.2 %collective-permute-start.2 = (f32[1,1280]{1,0:T(1,128)}, f32[1,1280]{1,0:T(1,128)S(1)}, u32[]{:S(2)}, u32[]{:S(2)}) collective-permute-start(f32[1,1280]{1,0:T(1,128)} %slice.68), channel_id=1, source_target_pairs={{0,1},{1,2},{2,3},{3,4},{4,5},{5,6},{6,7},{7,8},{8,9},{9,10},{10,1... | collective-permute-start | bytes 15368 | tf_op jit(solution)/shard_map/ppermute | solution.py:19
  57.8 13.1 %copy-start.60 = (s32[1,80]{1,0:T(1,128)S(1)}, s32[1,80]{1,0:T(1,128)}, u32[]{:S(2)}) copy-start(s32[1,80]{1,0:T(1,128)} %param.45) | copy-start | bytes 964
  57.8 14.2 %copy-start.55 = (s32[1,352]{1,0:T(1,128)S(1)}, s32[1,352]{1,0:T(1,128)}, u32[]{:S(2)}) copy-start(s32[1,352]{1,0:T(1,128)} %param.43) | copy-start | bytes 4228
  57.8 14.8 %copy-start.33 = (s32[6,128]{1,0:T(8,128)S(1)}, s32[6,128]{1,0:T(8,128)}, u32[]{:S(2)}) copy-start(s32[6,128]{1,0:T(8,128)} %param.38) | copy-start | bytes 9220
  58.6 27.0 %collective-permute-start.3 = (f32[1,1280]{1,0:T(1,128)}, f32[1,1280]{1,0:T(1,128)S(1)}, u32[]{:S(2)}, u32[]{:S(2)}) collective-permute-start(f32[1,1280]{1,0:T(1,128)} %slice.70), channel_id=1, source_target_pairs={{1,0},{2,1},{3,2},{4,3},{5,4},{6,5},{7,6},{8,7},{9,8},{10,9},{11,1... | collective-permute-start | bytes 15368 | tf_op jit(solution)/shard_map/ppermute | solution.py:20
  60.4 12.8 %copy-start.40 = (pred[352]{0:T(512)(128)(4,1)}, pred[352]{0:T(512)(128)(4,1)S(1)}, u32[]{:S(2)}) copy-start(pred[352]{0:T(512)(128)(4,1)S(1)} %compare_and_fusion.3) | copy-start | bytes 1060
  62.1 12.1 %copy-start.27 = (f32[75,128]{1,0:T(8,128)S(1)}, f32[75,128]{1,0:T(8,128)}, u32[]{:S(2)}) copy-start(f32[75,128]{1,0:T(8,128)} %param.34) | copy-start | bytes 115204
  62.9 22.8 %all-to-all-start = ((f32[80,16,22]{0,2,1:T(8,128)}), f32[80,16,22]{0,2,1:T(8,128)}, u32[]{:S(2)}, u32[]{:S(2)}) async-start(f32[80,16,22]{0,2,1:T(8,128)} %all_to_all.24), calls=%async_computation | async-start | bytes 393216 | tf_op jit(solution)/shard_map/all_to_all | solution.py:257
  85.8 12.0 %all-to-all-start.1 = ((f32[80,16,22]{0,2,1:T(8,128)}), f32[80,16,22]{0,2,1:T(8,128)S(1)}, u32[]{:S(2)}, u32[]{:S(2)}) async-start(f32[80,16,22]{0,2,1:T(8,128)} %all_to_all.26), calls=%async_computation.1 | async-start | bytes 393216 | tf_op jit(solution)/shard_map/all_to_all | solution.py:258
  111.4 48.0 %copy-start.20 = (f32[6,16,64,1]{2,1,0,3:T(8,128)S(1)}, f32[6,16,64,1]{2,1,0,3:T(8,128)}, u32[]{:S(2)}) copy-start(f32[6,16,64,1]{2,1,0,3:T(8,128)} %constant.85) | copy-start | bytes 73732
  167.6 11.3 %copy-start.49 = (pred[16]{0:T(512)(128)(4,1)S(1)}, pred[16]{0:T(512)(128)(4,1)}, u32[]{:S(2)}) copy-start(pred[16]{0:T(512)(128)(4,1)} %copy-done.48) | copy-start | bytes 52
  167.6 11.3 %copy-start.51 = (pred[16]{0:T(512)(128)(4,1)S(1)}, pred[16]{0:T(512)(128)(4,1)}, u32[]{:S(2)}) copy-start(pred[16]{0:T(512)(128)(4,1)} %copy-done.50) | copy-start | bytes 52
  171.3 9.9 %copy-start.14 = (f32[352,80]{1,0:T(8,128)S(1)}, f32[352,80]{1,0:T(8,128)}, u32[]{:S(2)}) copy-start(f32[352,80]{1,0:T(8,128)} %gather_fusion.12) | copy-start | bytes 337924
  171.3 9.9 %copy-start.41 = (pred[352]{0:T(512)(128)(4,1)S(1)}, pred[352]{0:T(512)(128)(4,1)}, u32[]{:S(2)}) copy-start(pred[352]{0:T(512)(128)(4,1)} %copy-done.40) | copy-start | bytes 1060
  171.3 16.6 %copy-start.53 = (pred[80]{0:T(512)(128)(4,1)S(1)}, pred[80]{0:T(512)(128)(4,1)}, u32[]{:S(2)}) copy-start(pred[80]{0:T(512)(128)(4,1)} %compare_and_fusion.2) | copy-start | bytes 244
  171.3 16.7 %copy-start.30 = (s32[1024]{0:T(1024)S(1)}, s32[1024]{0:T(1024)}, u32[]{:S(2)}) copy-start(s32[1024]{0:T(1024)} %copy-done.29) | copy-start | bytes 12292
  172.6 16.5 %copy-start.43 = (pred[352]{0:T(512)(128)(4,1)S(1)}, pred[352]{0:T(512)(128)(4,1)}, u32[]{:S(2)}) copy-start(pred[352]{0:T(512)(128)(4,1)} %compare_and_fusion.1) | copy-start | bytes 1060
  172.9 17.1 %collective-permute-start.4 = (f32[1,1280]{1,0:T(1,128)S(1)}, f32[1,1280]{1,0:T(1,128)S(1)}, u32[]{:S(2)}, u32[]{:S(2)}) collective-permute-start(f32[1,1280]{1,0:T(1,128)S(1)} %slice.73), channel_id=1, source_target_pairs={{0,16},{1,17},{2,18},{3,19},{4,20},{5,21},{6,22},{7,23},{8,24},{9,... | collective-permute-start | bytes 15368 | tf_op jit(solution)/shard_map/ppermute | solution.py:19
  174.4 15.8 %collective-permute-start.5 = (f32[1,1280]{1,0:T(1,128)S(1)}, f32[1,1280]{1,0:T(1,128)S(1)}, u32[]{:S(2)}, u32[]{:S(2)}) collective-permute-start(f32[1,1280]{1,0:T(1,128)S(1)} %slice.74), channel_id=1, source_target_pairs={{16,0},{17,1},{18,2},{19,3},{20,4},{21,5},{22,6},{23,7},{24,8},{25... | collective-permute-start | bytes 15368 | tf_op jit(solution)/shard_map/ppermute | solution.py:20
  179.2 11.1 %collective-permute-start.6 = (f32[1,1280]{1,0:T(1,128)S(1)}, f32[1,1280]{1,0:T(1,128)S(1)}, u32[]{:S(2)}, u32[]{:S(2)}) collective-permute-start(f32[1,1280]{1,0:T(1,128)S(1)} %slice.75), channel_id=1, source_target_pairs={{0,1},{1,2},{2,3},{3,4},{4,5},{5,6},{6,7},{7,8},{8,9},{9,10},{10,1... | collective-permute-start | bytes 15368 | tf_op jit(solution)/shard_map/ppermute | solution.py:19
  179.5 11.1 %collective-permute-start.7 = (f32[1,1280]{1,0:T(1,128)S(1)}, f32[1,1280]{1,0:T(1,128)S(1)}, u32[]{:S(2)}, u32[]{:S(2)}) collective-permute-start(f32[1,1280]{1,0:T(1,128)S(1)} %slice.76), channel_id=1, source_target_pairs={{1,0},{2,1},{3,2},{4,3},{5,4},{6,5},{7,6},{8,7},{9,8},{10,9},{11,1... | collective-permute-start | bytes 15368 | tf_op jit(solution)/shard_map/ppermute | solution.py:20
  182.1 11.8 %all-to-all-start.2 = ((f32[80,16,22]{0,2,1:T(8,128)}), f32[80,16,22]{0,2,1:T(8,128)S(1)}, u32[]{:S(2)}, u32[]{:S(2)}) async-start(f32[80,16,22]{0,2,1:T(8,128)} %all_to_all.28), calls=%async_computation.2 | async-start | bytes 393216 | tf_op jit(solution)/shard_map/all_to_all | solution.py:257
  189.1 11.9 %copy-start.23 = (f32[4,16,16,1]{2,1,0,3:T(8,128)S(1)}, f32[4,16,16,1]{2,1,0,3:T(8,128)}, u32[]{:S(2)}) copy-start(f32[4,16,16,1]{2,1,0,3:T(8,128)} %constant.86) | copy-start | bytes 12292
  189.1 11.9 %copy-start.24 = (f32[4,352]{1,0:T(4,128)S(1)}, f32[4,352]{1,0:T(4,128)}, u32[]{:S(2)}) copy-start(f32[4,352]{1,0:T(4,128)} %fusion.27) | copy-start | bytes 16900
  193.8 12.5 %all-to-all-start.3 = ((f32[80,16,22]{0,2,1:T(8,128)}), f32[80,16,22]{0,2,1:T(8,128)S(1)}, u32[]{:S(2)}, u32[]{:S(2)}) async-start(f32[80,16,22]{0,2,1:T(8,128)} %all_to_all.30), calls=%async_computation.3 | async-start | bytes 393216 | tf_op jit(solution)/shard_map/all_to_all | solution.py:258
  (41 other events, 124.0 us)
where the time goes:
time: 265 us; the launch traced here: 264 us
  blocking collectives  124 us (47%)
  starting transfers between devices  41.6 us (16%)
  local copies, waits for them, and re-layouts  40.4 us (15%)
  matrix products  24.4 us (9%)
  other arithmetic  12.4 us (5%)
  between operations  10.7 us (4%)
  waiting for transfers between devices  10.2 us (4%)
    psum x3, blocking collectives, merged_global(): return lax.psum(partial_values, ('gx', 'yz'))  124 us
    all_to_all x2, starting transfers between devices, on_device(): lax.all_to_all(fine_send, 'yz', split_axis=1, concat_axis=1, tiled=True)  13.7 us
    all_to_all x2, starting transfers between devices, on_device(): lax.all_to_all(outgoing, 'yz', split_axis=1, concat_axis=1, tiled=True)  12.6 us
    ppermute x4, starting transfers between devices, with_halo(): after = lax.ppermute(leading, axis, down)  12.6 us
    dot_general x2, matrix products, jacobian(): jnp.einsum('dabe,bne->dane', flux_blocks, nodal_view, precision=maximum_d...  7.32 us
    all_to_all x2, waiting for transfers between devices, on_device(): lax.all_to_all(outgoing, 'yz', split_axis=1, concat_axis=1, tiled=True)  7.04 us
    gather x4, local copies, waits for them, and re-layouts, on_device(): jnp.take(trace_table, near_index, axis=1, mode='fill', fill_value=0.0)  5.46 us
  transfers between devices with their start and end apart: 12, of which 3 were waited for; matrix products, arithmetic and copies ran while one was open for 10% of the time, Pallas kernels for 0%

commit v1 on v0

--- a/solution.py
+++ b/solution.py
@@ -7,6 +7,18 @@
 ITERS = 2
 maximum_depth = lax.Precision.HIGHEST
 epsilon = 1e-06
+
+
+def cut_along(shard, dim, size):
+    dims = shard.shape
+    parts = shard.reshape(*dims[:dim], size, dims[dim] // size, *dims[dim + 1 :])
+    return jnp.moveaxis(parts, dim, 0)
+
+
+def in_order(pieces, dim):
+    shape = list(pieces.shape[1:])
+    shape[dim] *= pieces.shape[0]
+    return jnp.moveaxis(pieces, 0, dim).reshape(shape)
 
 
 def with_halo(shard, sides, width, wrap):
@@ -254,7 +266,18 @@
         )
         coarse = jnp.take(own_faces, coarse_mortar_table_slot[0], axis=1)
         outgoing = jnp.take(coarse, incoming_mortar_index[0], axis=1, mode="fill", fill_value=0.0)
-        fine_recv = lax.all_to_all(fine_send, "yz", split_axis=1, concat_axis=1, tiled=True)
+        length_2, index = (lax.axis_size("yz"), lax.axis_index("yz"))
+        blocks = cut_along(fine_send, 1, length_2)
+        outs = [blocks[index]]
+        for step in range(1, length_2):
+            sent = blocks[(index + step) % length_2]
+            outs.append(
+                lax.ppermute(
+                    sent, "yz", [(i_2, (i_2 + step) % length_2) for i_2 in range(length_2)]
+                )
+            )
+        blocks = jnp.stack(outs)[(index - jnp.arange(length_2)) % length_2]
+        fine_recv = in_order(blocks, 1)
         coarse_cols = lax.all_to_all(outgoing, "yz", split_axis=1, concat_axis=1, tiled=True)
         hang_sum = mortar_sums(
             fine_recv, incoming_mortar_index[0], incoming_quadrant_index[0], projection, hang_count

time: 265 us -> 297 us (1.12)
  starting transfers between devices: 41.6 us -> 73 us
  waiting for transfers between devices: 10.2 us -> 2.82 us
  local copies, waits for them, and re-layouts: 40.4 us -> 47.2 us
    ppermute x0 -> x30, starting transfers between devices: none -> 40.1 us  [on_device(): lax.ppermute(sent, 'yz', [(i_2, (i_2 + step) % length_2) for i_2 in range...]
    all_to_all x2 -> x0, starting transfers between devices: 13.7 us -> none  [on_device(): lax.all_to_all(fine_send, 'yz', split_axis=1, concat_axis=1, tiled=True)]
    all_to_all x2, waiting for transfers between devices: 7.04 us -> 0.01 us  [on_device(): lax.all_to_all(outgoing, 'yz', split_axis=1, concat_axis=1, tiled=True)]
    all_to_all x2, starting transfers between devices: 12.6 us -> 17.6 us  [on_device(): lax.all_to_all(outgoing, 'yz', split_axis=1, concat_axis=1, tiled=True)]
    all_to_all x4 -> x0, local copies, waits for them, and re-layouts: 3.84 us -> none  [on_device(): lax.all_to_all(fine_send, 'yz', split_axis=1, concat_axis=1, tiled=True)]
    all_to_all x2 -> x0, waiting for transfers between devices: 3.11 us -> none  [on_device(): lax.all_to_all(fine_send, 'yz', split_axis=1, concat_axis=1, tiled=True)]
  transfers between devices with their start and end apart: 12 -> 40, of which waited for: 3 -> 6; matrix products, arithmetic and copies ran while one was open for 10% -> 10% of each run, Pallas kernels for 0% -> 0%
where the time goes in v1:
time: 297 us; the launch traced here: 295 us
  blocking collectives  124 us (42%)
  starting transfers between devices  73 us (25%)
  local copies, waits for them, and re-layouts  47.2 us (16%)
  matrix products  23 us (8%)
  other arithmetic  12.5 us (4%)
  between operations  11.8 us (4%)
    psum x3, blocking collectives, merged_global(): return lax.psum(partial_values, ('gx', 'yz'))  124 us
    ppermute x30, starting transfers between devices, on_device(): lax.ppermute(sent, 'yz', [(i_2, (i_2 + step) % length_2) for i_2 in range...  40.1 us
    all_to_all x2, starting transfers between devices, on_device(): lax.all_to_all(outgoing, 'yz', split_axis=1, concat_axis=1, tiled=True)  17.6 us
    ppermute x4, starting transfers between devices, with_halo(): after = lax.ppermute(leading, axis, down)  12.7 us
    dot_general x2, matrix products, jacobian(): jnp.einsum('dabe,bne->dane', flux_blocks, nodal_view, precision=maximum_d...  7.31 us
  transfers between devices with their start and end apart: 40, of which 6 were waited for; matrix products, arithmetic and copies ran while one was open for 10% of the time, Pallas kernels for 0%

profile of v1, /device:TPU:14, one launch (start us, length us, event | category | flops | bytes accessed | tf_op | source)
XLA Modules:
  0.0 294.8 jit_solution(17781276768996939622)
XLA Ops:
  1.0 1.5 convolution_multiply_fusion
  2.6 2.2 multiply_reduce_fusion.3
  4.8 40.6 %psum.21 = f32[1]{0:T(128)} all-reduce(f32[1]{0:T(128)} %bitcast), channel_id=1, replica_groups=mesh['gx'=2,'yz'=16] {'gx','yz'}, use_global_device_ids=true, to_apply=%region_1.0 | all-reduce | flops 1 | bytes 8 | tf_op jit(solution)/shard_map/psum | solution.py:213
  51.8 4.5 %collective-permute-start.1 = (f32[1,1280]{1,0:T(1,128)}, f32[1,1280]{1,0:T(1,128)S(1)}, u32[]{:S(2)}, u32[]{:S(2)}) collective-permute-start(f32[1,1280]{1,0:T(1,128)} %slice.66), channel_id=1, source_target_pairs={{16,0},{17,1},{18,2},{19,3},{20,4},{21,5},{22,6},{23,7},{24,8},{25... | collective-permute-start | bytes 15368 | tf_op jit(solution)/shard_map/ppermute | solution.py:32
  59.2 1.7 collective-permute-start.3
  67.8 9.2 %all-to-all-start = ((f32[80,16,22]{0,2,1:T(8,128)}), f32[80,16,22]{0,2,1:T(8,128)}, u32[]{:S(2)}, u32[]{:S(2)}) async-start(f32[80,16,22]{0,2,1:T(8,128)} %all_to_all.12), calls=%async_computation | async-start | bytes 393216 | tf_op jit(solution)/shard_map/all_to_all | solution.py:281
  79.4 3.7 %convolution_bitcast_fusion.1 = f32[3,5,64,128]{2,1,0,3:T(8,128)S(1)} fusion(f32[5,64,128,1]{1,0,3,2:T(8,128)} %copy.178, f32[3,5,5,128]{2,1,0,3:T(8,128)S(1)} %copy.128), kind=kOutput, calls=%fused_computation.19 | convolution fusion | flops 7372800 | bytes 693760 | tf_op jit(solution)/shard_map/dabe,bne->dane/dot_general | solution.py:129
  83.1 2.0 convolution_bitcast_fusion.13
  91.6 2.4 collective-permute-start.9
  94.7 1.8 collective-permute-start.10
  97.9 2.3 collective-permute-start.13
  100.2 2.8 collective-permute-start.14
  105.2 2.3 collective-permute-start.18
  113.1 2.1 copy.142
  117.3 2.6 gather_fusion.9
  128.4 41.9 %psum.22 = f32[2]{0:T(128)S(1)} all-reduce(f32[2]{0:T(128)S(1)} %pad_maximum_fusion), channel_id=1, replica_groups=mesh['gx'=2,'yz'=16] {'gx','yz'}, use_global_device_ids=true, to_apply=%region_6.12 | all-reduce | flops 2 | bytes 16 | tf_op jit(solution)/shard_map/psum | solution.py:213
  177.6 1.6 gather_fusion.14
  179.2 1.7 select_bitcast_fusion.1
  180.9 1.6 reshape.284
  183.9 1.5 dynamic-slice_bitcast_fusion
  187.9 3.7 %convolution_bitcast_fusion = f32[3,5,64,128]{2,1,0,3:T(8,128)S(1)} fusion(f32[5,64,128,1]{1,0,3,2:T(8,128)} %copy.185, f32[3,5,5,128]{2,1,0,3:T(8,128)S(1)} %copy.128), kind=kOutput, calls=%fused_computation.18 | convolution fusion | flops 7372800 | bytes 693760 | tf_op jit(solution)/shard_map/dabe,bne->dane/dot_general | solution.py:129
  194.8 4.7 %collective-permute-start.20 = (f32[1,1280]{1,0:T(1,128)S(1)}, f32[1,1280]{1,0:T(1,128)S(1)}, u32[]{:S(2)}, u32[]{:S(2)}) collective-permute-start(f32[1,1280]{1,0:T(1,128)S(1)} %slice.74), channel_id=1, source_target_pairs={{16,0},{17,1},{18,2},{19,3},{20,4},{21,5},{22,6},{23,7},{24,8},{25... | collective-permute-start | bytes 15368 | tf_op jit(solution)/shard_map/ppermute | solution.py:32
  200.1 1.8 collective-permute-start.22
  203.9 8.4 %all-to-all-start.1 = ((f32[80,16,22]{0,2,1:T(8,128)}), f32[80,16,22]{0,2,1:T(8,128)S(1)}, u32[]{:S(2)}, u32[]{:S(2)}) async-start(f32[80,16,22]{0,2,1:T(8,128)} %all_to_all.14), calls=%async_computation.1 | async-start | bytes 393216 | tf_op jit(solution)/shard_map/all_to_all | solution.py:281
  217.8 2.4 collective-permute-start.28
  220.3 1.9 collective-permute-start.29
  223.5 2.3 collective-permute-start.32
  225.8 2.8 collective-permute-start.33
  230.8 2.3 collective-permute-start.37
  238.4 1.6 gather_fusion.17
  243.0 2.1 pad_maximum_fusion.1
  245.1 41.9 %psum.23 = f32[3]{0:T(128)S(1)} all-reduce(f32[3]{0:T(128)S(1)} %pad_maximum_fusion.1), channel_id=1, replica_groups=mesh['gx'=2,'yz'=16] {'gx','yz'}, use_global_device_ids=true, to_apply=%region_12.18 | all-reduce | flops 3 | bytes 24 | tf_op jit(solution)/shard_map/psum | solution.py:213
  (423 shorter events, 77.3 us)
Async XLA Ops:
  49.0 36.7 %collective-permute-start = (f32[1,1280]{1,0:T(1,128)}, f32[1,1280]{1,0:T(1,128)S(1)}, u32[]{:S(2)}, u32[]{:S(2)}) collective-permute-start(f32[1,1280]{1,0:T(1,128)} %slice.64), channel_id=1, source_target_pairs={{0,16},{1,17},{2,18},{3,19},{4,20},{5,21},{6,22},{7,23},{8,24},{9,... | collective-permute-start | bytes 15368 | tf_op jit(solution)/shard_map/ppermute | solution.py:31
  51.8 35.5 %collective-permute-start.1 = (f32[1,1280]{1,0:T(1,128)}, f32[1,1280]{1,0:T(1,128)S(1)}, u32[]{:S(2)}, u32[]{:S(2)}) collective-permute-start(f32[1,1280]{1,0:T(1,128)} %slice.66), channel_id=1, source_target_pairs={{16,0},{17,1},{18,2},{19,3},{20,4},{21,5},{22,6},{23,7},{24,8},{25... | collective-permute-start | bytes 15368 | tf_op jit(solution)/shard_map/ppermute | solution.py:32
  57.8 30.7 %collective-permute-start.2 = (f32[1,1280]{1,0:T(1,128)}, f32[1,1280]{1,0:T(1,128)S(1)}, u32[]{:S(2)}, u32[]{:S(2)}) collective-permute-start(f32[1,1280]{1,0:T(1,128)} %slice.68), channel_id=1, source_target_pairs={{0,1},{1,2},{2,3},{3,4},{4,5},{5,6},{6,7},{7,8},{8,9},{9,10},{10,1... | collective-permute-start | bytes 15368 | tf_op jit(solution)/shard_map/ppermute | solution.py:31
  59.2 30.9 %collective-permute-start.3 = (f32[1,1280]{1,0:T(1,128)}, f32[1,1280]{1,0:T(1,128)}, u32[]{:S(2)}, u32[]{:S(2)}) collective-permute-start(f32[1,1280]{1,0:T(1,128)} %slice.70), channel_id=1, source_target_pairs={{1,0},{2,1},{3,2},{4,3},{5,4},{6,5},{7,6},{8,7},{9,8},{10,9},{11,1... | collective-permute-start | bytes 15368 | tf_op jit(solution)/shard_map/ppermute | solution.py:32
  64.5 27.1 %collective-permute-start.4 = (f32[80,22]{0,1:T(8,128)}, f32[80,22]{0,1:T(8,128)}, u32[]{:S(2)}, u32[]{:S(2)}) collective-permute-start(f32[80,22]{0,1:T(8,128)} %get-tuple-element.52), channel_id=1, source_target_pairs={{0,1},{1,2},{2,3},{3,4},{4,5},{5,6},{6,7},{7,8},{8,9},{9,10},{10,1... | collective-permute-start | bytes 21128 | tf_op jit(solution)/shard_map/ppermute | solution.py:275
  67.8 45.3 %all-to-all-start = ((f32[80,16,22]{0,2,1:T(8,128)}), f32[80,16,22]{0,2,1:T(8,128)}, u32[]{:S(2)}, u32[]{:S(2)}) async-start(f32[80,16,22]{0,2,1:T(8,128)} %all_to_all.12), calls=%async_computation | async-start | bytes 393216 | tf_op jit(solution)/shard_map/all_to_all | solution.py:281
  85.7 9.0 %collective-permute-start.5 = (f32[80,22]{0,1:T(8,128)}, f32[80,22]{0,1:T(8,128)S(1)}, u32[]{:S(2)}, u32[]{:S(2)}) collective-permute-start(f32[80,22]{0,1:T(8,128)} %get-tuple-element.51), channel_id=1, source_target_pairs={{0,2},{1,3},{2,4},{3,5},{4,6},{5,7},{6,8},{7,9},{8,10},{9,11},{10,... | collective-permute-start | bytes 21128 | tf_op jit(solution)/shard_map/ppermute | solution.py:275
  87.3 9.2 %collective-permute-start.6 = (f32[80,22]{0,1:T(8,128)}, f32[80,22]{0,1:T(8,128)S(1)}, u32[]{:S(2)}, u32[]{:S(2)}) collective-permute-start(f32[80,22]{0,1:T(8,128)} %get-tuple-element.50), channel_id=1, source_target_pairs={{0,3},{1,4},{2,5},{3,6},{4,7},{5,8},{6,9},{7,10},{8,11},{9,12},{10... | collective-permute-start | bytes 21128 | tf_op jit(solution)/shard_map/ppermute | solution.py:275
  88.4 8.8 %collective-permute-start.7 = (f32[80,22]{0,1:T(8,128)S(1)}, f32[80,22]{0,1:T(8,128)S(1)}, u32[]{:S(2)}, u32[]{:S(2)}) collective-permute-start(f32[80,22]{0,1:T(8,128)S(1)} %copy-done.57), channel_id=1, source_target_pairs={{0,4},{1,5},{2,6},{3,7},{4,8},{5,9},{6,10},{7,11},{8,12},{9,13},{1... | collective-permute-start | bytes 21128 | tf_op jit(solution)/shard_map/ppermute | solution.py:275
  90.1 7.8 %collective-permute-start.8 = (f32[80,22]{0,1:T(8,128)S(1)}, f32[80,22]{0,1:T(8,128)S(1)}, u32[]{:S(2)}, u32[]{:S(2)}) collective-permute-start(f32[80,22]{0,1:T(8,128)S(1)} %copy-done.56), channel_id=1, source_target_pairs={{0,5},{1,6},{2,7},{3,8},{4,9},{5,10},{6,11},{7,12},{8,13},{9,14},{... | collective-permute-start | bytes 21128 | tf_op jit(solution)/shard_map/ppermute | solution.py:275
  91.6 8.6 %collective-permute-start.9 = (f32[80,22]{0,1:T(8,128)S(1)}, f32[80,22]{0,1:T(8,128)S(1)}, u32[]{:S(2)}, u32[]{:S(2)}) collective-permute-start(f32[80,22]{0,1:T(8,128)S(1)} %copy-done.54), channel_id=1, source_target_pairs={{0,6},{1,7},{2,8},{3,9},{4,10},{5,11},{6,12},{7,13},{8,14},{9,15},... | collective-permute-start | bytes 21128 | tf_op jit(solution)/shard_map/ppermute | solution.py:275
  94.7 8.3 %collective-permute-start.10 = (f32[80,22]{0,1:T(8,128)S(1)}, f32[80,22]{0,1:T(8,128)S(1)}, u32[]{:S(2)}, u32[]{:S(2)}) collective-permute-start(f32[80,22]{0,1:T(8,128)S(1)} %copy-done.52), channel_id=1, source_target_pairs={{0,7},{1,8},{2,9},{3,10},{4,11},{5,12},{6,13},{7,14},{8,15},{9,0},... | collective-permute-start | bytes 21128 | tf_op jit(solution)/shard_map/ppermute | solution.py:275
  96.5 7.1 %collective-permute-start.11 = (f32[80,22]{0,1:T(8,128)S(1)}, f32[80,22]{0,1:T(8,128)S(1)}, u32[]{:S(2)}, u32[]{:S(2)}) collective-permute-start(f32[80,22]{0,1:T(8,128)S(1)} %copy-done.50), channel_id=1, source_target_pairs={{0,8},{1,9},{2,10},{3,11},{4,12},{5,13},{6,14},{7,15},{8,0},{9,1},... | collective-permute-start | bytes 21128 | tf_op jit(solution)/shard_map/ppermute | solution.py:275
  97.2 6.5 %collective-permute-start.12 = (f32[80,22]{0,1:T(8,128)S(1)}, f32[80,22]{0,1:T(8,128)S(1)}, u32[]{:S(2)}, u32[]{:S(2)}) collective-permute-start(f32[80,22]{0,1:T(8,128)S(1)} %copy-done.48), channel_id=1, source_target_pairs={{0,9},{1,10},{2,11},{3,12},{4,13},{5,14},{6,15},{7,0},{8,1},{9,2},... | collective-permute-start | bytes 21128 | tf_op jit(solution)/shard_map/ppermute | solution.py:275
  97.9 7.4 %collective-permute-start.13 = (f32[80,22]{0,1:T(8,128)S(1)}, f32[80,22]{0,1:T(8,128)S(1)}, u32[]{:S(2)}, u32[]{:S(2)}) collective-permute-start(f32[80,22]{0,1:T(8,128)S(1)} %copy-done.46), channel_id=1, source_target_pairs={{0,10},{1,11},{2,12},{3,13},{4,14},{5,15},{6,0},{7,1},{8,2},{9,3},... | collective-permute-start | bytes 21128 | tf_op jit(solution)/shard_map/ppermute | solution.py:275
  100.2 7.3 %collective-permute-start.14 = (f32[80,22]{0,1:T(8,128)S(1)}, f32[80,22]{0,1:T(8,128)S(1)}, u32[]{:S(2)}, u32[]{:S(2)}) collective-permute-start(f32[80,22]{0,1:T(8,128)S(1)} %copy-done.44), channel_id=1, source_target_pairs={{0,11},{1,12},{2,13},{3,14},{4,15},{5,0},{6,1},{7,2},{8,3},{9,4},{... | collective-permute-start | bytes 21128 | tf_op jit(solution)/shard_map/ppermute | solution.py:275
  193.2 19.1 %collective-permute-start.19 = (f32[1,1280]{1,0:T(1,128)S(1)}, f32[1,1280]{1,0:T(1,128)S(1)}, u32[]{:S(2)}, u32[]{:S(2)}) collective-permute-start(f32[1,1280]{1,0:T(1,128)S(1)} %slice.73), channel_id=1, source_target_pairs={{0,16},{1,17},{2,18},{3,19},{4,20},{5,21},{6,22},{7,23},{8,24},{9,... | collective-permute-start | bytes 15368 | tf_op jit(solution)/shard_map/ppermute | solution.py:31
  194.8 19.2 %collective-permute-start.20 = (f32[1,1280]{1,0:T(1,128)S(1)}, f32[1,1280]{1,0:T(1,128)S(1)}, u32[]{:S(2)}, u32[]{:S(2)}) collective-permute-start(f32[1,1280]{1,0:T(1,128)S(1)} %slice.74), channel_id=1, source_target_pairs={{16,0},{17,1},{18,2},{19,3},{20,4},{21,5},{22,6},{23,7},{24,8},{25... | collective-permute-start | bytes 15368 | tf_op jit(solution)/shard_map/ppermute | solution.py:32
  199.7 15.4 %collective-permute-start.21 = (f32[1,1280]{1,0:T(1,128)S(1)}, f32[1,1280]{1,0:T(1,128)S(1)}, u32[]{:S(2)}, u32[]{:S(2)}) collective-permute-start(f32[1,1280]{1,0:T(1,128)S(1)} %slice.75), channel_id=1, source_target_pairs={{0,1},{1,2},{2,3},{3,4},{4,5},{5,6},{6,7},{7,8},{8,9},{9,10},{10,1... | collective-permute-start | bytes 15368 | tf_op jit(solution)/shard_map/ppermute | solution.py:31
  200.1 16.7 %collective-permute-start.22 = (f32[1,1280]{1,0:T(1,128)S(1)}, f32[1,1280]{1,0:T(1,128)S(1)}, u32[]{:S(2)}, u32[]{:S(2)}) collective-permute-start(f32[1,1280]{1,0:T(1,128)S(1)} %slice.76), channel_id=1, source_target_pairs={{1,0},{2,1},{3,2},{4,3},{5,4},{6,5},{7,6},{8,7},{9,8},{10,9},{11,1... | collective-permute-start | bytes 15368 | tf_op jit(solution)/shard_map/ppermute | solution.py:32
  201.9 15.9 %collective-permute-start.23 = (f32[80,22]{0,1:T(8,128)S(1)}, f32[80,22]{0,1:T(8,128)S(1)}, u32[]{:S(2)}, u32[]{:S(2)}) collective-permute-start(f32[80,22]{0,1:T(8,128)S(1)} %copy-done.55), channel_id=1, source_target_pairs={{0,1},{1,2},{2,3},{3,4},{4,5},{5,6},{6,7},{7,8},{8,9},{9,10},{10,1... | collective-permute-start | bytes 21128 | tf_op jit(solution)/shard_map/ppermute | solution.py:275
  203.9 33.1 %all-to-all-start.1 = ((f32[80,16,22]{0,2,1:T(8,128)}), f32[80,16,22]{0,2,1:T(8,128)S(1)}, u32[]{:S(2)}, u32[]{:S(2)}) async-start(f32[80,16,22]{0,2,1:T(8,128)} %all_to_all.14), calls=%async_computation.1 | async-start | bytes 393216 | tf_op jit(solution)/shard_map/all_to_all | solution.py:281
  212.3 7.9 %collective-permute-start.24 = (f32[80,22]{0,1:T(8,128)S(1)}, f32[80,22]{0,1:T(8,128)S(1)}, u32[]{:S(2)}, u32[]{:S(2)}) collective-permute-start(f32[80,22]{0,1:T(8,128)S(1)} %copy-done.53), channel_id=1, source_target_pairs={{0,2},{1,3},{2,4},{3,5},{4,6},{5,7},{6,8},{7,9},{8,10},{9,11},{10,... | collective-permute-start | bytes 21128 | tf_op jit(solution)/shard_map/ppermute | solution.py:275
  214.0 8.1 %collective-permute-start.25 = (f32[80,22]{0,1:T(8,128)S(1)}, f32[80,22]{0,1:T(8,128)S(1)}, u32[]{:S(2)}, u32[]{:S(2)}) collective-permute-start(f32[80,22]{0,1:T(8,128)S(1)} %copy-done.51), channel_id=1, source_target_pairs={{0,3},{1,4},{2,5},{3,6},{4,7},{5,8},{6,9},{7,10},{8,11},{9,12},{10... | collective-permute-start | bytes 21128 | tf_op jit(solution)/shard_map/ppermute | solution.py:275
  215.1 7.6 %collective-permute-start.26 = (f32[80,22]{0,1:T(8,128)S(1)}, f32[80,22]{0,1:T(8,128)S(1)}, u32[]{:S(2)}, u32[]{:S(2)}) collective-permute-start(f32[80,22]{0,1:T(8,128)S(1)} %copy-done.49), channel_id=1, source_target_pairs={{0,4},{1,5},{2,6},{3,7},{4,8},{5,9},{6,10},{7,11},{8,12},{9,13},{1... | collective-permute-start | bytes 21128 | tf_op jit(solution)/shard_map/ppermute | solution.py:275
  216.8 6.7 %collective-permute-start.27 = (f32[80,22]{0,1:T(8,128)S(1)}, f32[80,22]{0,1:T(8,128)S(1)}, u32[]{:S(2)}, u32[]{:S(2)}) collective-permute-start(f32[80,22]{0,1:T(8,128)S(1)} %copy-done.47), channel_id=1, source_target_pairs={{0,5},{1,6},{2,7},{3,8},{4,9},{5,10},{6,11},{7,12},{8,13},{9,14},{... | collective-permute-start | bytes 21128 | tf_op jit(solution)/shard_map/ppermute | solution.py:275
  217.8 8.0 %collective-permute-start.28 = (f32[80,22]{0,1:T(8,128)S(1)}, f32[80,22]{0,1:T(8,128)S(1)}, u32[]{:S(2)}, u32[]{:S(2)}) collective-permute-start(f32[80,22]{0,1:T(8,128)S(1)} %copy-done.45), channel_id=1, source_target_pairs={{0,6},{1,7},{2,8},{3,9},{4,10},{5,11},{6,12},{7,13},{8,14},{9,15},... | collective-permute-start | bytes 21128 | tf_op jit(solution)/shard_map/ppermute | solution.py:275
  220.3 8.3 %collective-permute-start.29 = (f32[80,22]{0,1:T(8,128)S(1)}, f32[80,22]{0,1:T(8,128)S(1)}, u32[]{:S(2)}, u32[]{:S(2)}) collective-permute-start(f32[80,22]{0,1:T(8,128)S(1)} %copy-done.43), channel_id=1, source_target_pairs={{0,7},{1,8},{2,9},{3,10},{4,11},{5,12},{6,13},{7,14},{8,15},{9,0},... | collective-permute-start | bytes 21128 | tf_op jit(solution)/shard_map/ppermute | solution.py:275
  222.1 7.1 %collective-permute-start.30 = (f32[80,22]{0,1:T(8,128)S(1)}, f32[80,22]{0,1:T(8,128)S(1)}, u32[]{:S(2)}, u32[]{:S(2)}) collective-permute-start(f32[80,22]{0,1:T(8,128)S(1)} %copy-done.41), channel_id=1, source_target_pairs={{0,8},{1,9},{2,10},{3,11},{4,12},{5,13},{6,14},{7,15},{8,0},{9,1},... | collective-permute-start | bytes 21128 | tf_op jit(solution)/shard_map/ppermute | solution.py:275
  222.8 6.5 %collective-permute-start.31 = (f32[80,22]{0,1:T(8,128)S(1)}, f32[80,22]{0,1:T(8,128)S(1)}, u32[]{:S(2)}, u32[]{:S(2)}) collective-permute-start(f32[80,22]{0,1:T(8,128)S(1)} %copy-done.40), channel_id=1, source_target_pairs={{0,9},{1,10},{2,11},{3,12},{4,13},{5,14},{6,15},{7,0},{8,1},{9,2},... | collective-permute-start | bytes 21128 | tf_op jit(solution)/shard_map/ppermute | solution.py:275
  223.5 7.4 %collective-permute-start.32 = (f32[80,22]{0,1:T(8,128)S(1)}, f32[80,22]{0,1:T(8,128)S(1)}, u32[]{:S(2)}, u32[]{:S(2)}) collective-permute-start(f32[80,22]{0,1:T(8,128)S(1)} %copy-done.39), channel_id=1, source_target_pairs={{0,10},{1,11},{2,12},{3,13},{4,14},{5,15},{6,0},{7,1},{8,2},{9,3},... | collective-permute-start | bytes 21128 | tf_op jit(solution)/shard_map/ppermute | solution.py:275
  225.8 7.3 %collective-permute-start.33 = (f32[80,22]{0,1:T(8,128)S(1)}, f32[80,22]{0,1:T(8,128)S(1)}, u32[]{:S(2)}, u32[]{:S(2)}) collective-permute-start(f32[80,22]{0,1:T(8,128)S(1)} %copy-done.38), channel_id=1, source_target_pairs={{0,11},{1,12},{2,13},{3,14},{4,15},{5,0},{6,1},{7,2},{8,3},{9,4},{... | collective-permute-start | bytes 21128 | tf_op jit(solution)/shard_map/ppermute | solution.py:275
  (93 other events, 1109.5 us)
